TPU v7x, 32 devices: a whole 2x2x4 slice. The times are simulated.
32 devices in a mesh: img: 8 (over z, x), head: 4 (over y, core).
Axes of the slice: x: 2, y: 2, z: 4, core: 2. Of those that a mesh axis runs over, the one named last changes fastest.
Arguments:
- inputs: bfloat16 [2048, 1280], P('img'), may hold values from -6 to 6
- middle: bfloat16 [2048, 1280], P('img'), may hold values from -6 to 6
- out_grad: bfloat16 [2048, 1280], P('img'), may hold values from -6 to 6
- cached_maps: bfloat16 [8, 16, 256, 256], P('img', 'head'), may hold values from 0 to 1, as said below
- w_value: bfloat16 [1280, 1280], P(None, 'head'), may hold values from -0.15625 to 0.15625
- w_out: bfloat16 [1280, 1280], P('head'), may hold values from -0.15625 to 0.15625
- w_up: bfloat16 [1280, 2560], P(None, 'head'), may hold values from -0.15625 to 0.15625
- w_down: bfloat16 [2560, 1280], P('head'), may hold values from -0.125 to 0.125
Outputs:
- in_grad: bfloat16 [2048, 1280], P(('img', 'head'))
- grad_value: float32 [1280, 1280], P('img', 'head')
- grad_out: float32 [1280, 1280], P('head', 'img')
- grad_up: float32 [1280, 2560], P('img', 'head')
- grad_down: float32 [2560, 1280], P('head', 'img')
Inputs may be any that keep to these rules, and one draw needn't show every extreme that they name: `cached_maps`: every row of every map is positive and sums to one up to rounding.
All inputs are finite; a program needn't handle non-finite values.
Results may differ from a plain program's by a relative error of at most 0.0069.
Values may be sent and summed in bfloat16 or wider, within the bound.
A program may use at most 128 MiB of HBM per device.

v0:
```python
import jax
import jax.numpy as jnp
from jax import lax
from jax.sharding import PartitionSpec as P


def norm_rows(rows):
    centre = rows - jnp.mean(rows, axis=-1, keepdims=True)
    spread = jnp.mean(centre * centre, axis=-1, keepdims=True)
    return centre * lax.rsqrt(spread + 1e-06)


def norm_back(rows, grad):
    centre = rows - jnp.mean(rows, axis=-1, keepdims=True)
    factor = lax.rsqrt(jnp.mean(centre * centre, axis=-1, keepdims=True) + 1e-06)
    normed = centre * factor
    return factor * (
        grad
        - jnp.mean(grad, axis=-1, keepdims=True)
        - normed * jnp.mean(grad * normed, axis=-1, keepdims=True)
    )


def gelu_tanh(pre):
    return jax.nn.gelu(pre, approximate=True)


def on_device(inputs, middle, out_grad, cached_maps, w_value, w_out, w_up, w_down):
    tok_rows = inputs.shape[0]
    heads_here = cached_maps.shape[1]
    share = tok_rows // lax.axis_size("head")
    first = lax.axis_index("head") * share
    maps_here = cached_maps[0]
    normed_in = norm_rows(inputs.astype(jnp.float32)).astype(jnp.bfloat16)
    values = jnp.dot(normed_in, w_value, preferred_element_type=jnp.float32).astype(jnp.bfloat16)
    head_size = values.shape[1] // heads_here
    attended = jnp.einsum(
        "htk,khd->thd",
        maps_here,
        values.reshape(tok_rows, heads_here, head_size),
        preferred_element_type=jnp.float32,
    )
    attended = attended.astype(jnp.bfloat16).reshape(tok_rows, -1)
    middle_f = middle.astype(jnp.float32)
    normed_mid = norm_rows(middle_f).astype(jnp.bfloat16)
    pre = jnp.dot(normed_mid, w_up, preferred_element_type=jnp.float32)
    hidden = gelu_tanh(pre).astype(jnp.bfloat16)
    hidden_grad = jnp.einsum("td,fd->tf", out_grad, w_down, preferred_element_type=jnp.float32)
    pre_grad = jax.vjp(gelu_tanh, pre)[1](hidden_grad)[0].astype(jnp.bfloat16)
    down_term = jnp.einsum("tf,td->fd", hidden, out_grad, preferred_element_type=jnp.float32)
    mid_part = jnp.einsum("tf,df->td", pre_grad, w_up, preferred_element_type=jnp.float32)
    out_rows = lax.dynamic_slice_in_dim(out_grad, first, share, 0).astype(jnp.float32)
    mid_share = lax.psum_scatter(mid_part, "head", scatter_dimension=0, tiled=True)
    mid_own = out_rows + norm_back(lax.dynamic_slice_in_dim(middle_f, first, share, 0), mid_share)
    mid_grad_b = lax.all_gather(mid_own.astype(jnp.bfloat16), "head", axis=0, tiled=True)
    outproj_term = jnp.einsum("te,td->ed", attended, mid_grad_b, preferred_element_type=jnp.float32)
    att_grad = jnp.einsum(
        "td,ed->te", mid_grad_b, w_out, preferred_element_type=jnp.float32
    ).astype(jnp.bfloat16)
    value_grad = jnp.einsum(
        "htk,thd->khd",
        maps_here,
        att_grad.reshape(tok_rows, heads_here, head_size),
        preferred_element_type=jnp.float32,
    )
    value_grad = value_grad.astype(jnp.bfloat16).reshape(tok_rows, -1)
    input_part = jnp.einsum("te,de->td", value_grad, w_value, preferred_element_type=jnp.float32)
    inputs_own = lax.dynamic_slice_in_dim(inputs, first, share, 0).astype(jnp.float32)
    input_share = lax.psum_scatter(input_part, "head", scatter_dimension=0, tiled=True)
    in_grad = (mid_own + norm_back(inputs_own, input_share)).astype(jnp.bfloat16)
    picked = normed_mid
    up_term = jnp.einsum("tr,tf->rf", picked, pre_grad, preferred_element_type=jnp.float32)
    picked = normed_in
    value_term = jnp.einsum("tr,te->re", picked, value_grad, preferred_element_type=jnp.float32)
    grad_down, grad_out = (
        lax.psum_scatter(down_term, "img", scatter_dimension=1, tiled=True),
        lax.psum_scatter(outproj_term, "img", scatter_dimension=1, tiled=True),
    )
    grad_up, grad_value = (
        lax.psum_scatter(up_term, "img", scatter_dimension=0, tiled=True),
        lax.psum_scatter(value_term, "img", scatter_dimension=0, tiled=True),
    )
    return (in_grad, grad_value, grad_out, grad_up, grad_down)


def solution(mesh):
    return jax.shard_map(
        on_device,
        mesh=mesh,
        in_specs=(
            P("img", None),
            P("img", None),
            P("img", None),
            P("img", "head", None, None),
            P(None, "head"),
            P("head", None),
            P(None, "head"),
            P("head", None),
        ),
        out_specs=(
            P(("img", "head"), None),
            P("img", "head"),
            P("head", "img"),
            P("img", "head"),
            P("head", "img"),
        ),
        check_vma=False,
    )
```

profile of v0, /device:TPU:0, one launch (start us, length us, event | category | flops | bytes accessed | tf_op | source)
XLA Modules:
  0.0 395.1 jit_solution(3205859704199914884)
XLA Ops:
  7.2 0.0 reduce-scatter.7.cloned.1.call-start
  7.2 1.4 convert_reduce_fusion.1
  8.7 1.4 multiply_reduce_fusion
  10.1 2.2 fusion.40
  12.3 1.8 fusion.10
  14.1 0.7 copy-done.10
  14.9 1.8 fusion.41
  16.7 0.0 reduce-scatter.9.cloned.1.call-start
  16.7 1.1 convert_element_type.49
  17.9 1.1 dynamic-slice_reduce_fusion
  19.0 1.2 multiply_reduce_fusion.2
  20.2 25.8 %reduce-scatter.7.cloned.1.call-done = f32[64,1280]{1,0:T(8,128)} async-done(((f32[256,1280]{1,0:T(8,128)}), f32[64,1280]{1,0:T(8,128)}) %reduce-scatter.7.cloned.1.call-update) | async-done | bytes 327696 | tf_op jit(solution)/shard_map/reduce_scatter | solution.py:53
  46.0 1.4 fusion.38
  47.4 2.0 fusion.39
  49.4 7.4 %all_gather.3 = bf16[256,1280]{1,0:T(8,128)(2,1)S(1)} all-gather(bf16[64,1280]{1,0:T(8,128)(2,1)S(1)} %get-tuple-element.9), channel_id=1, replica_groups=mesh['img'=8,'head'=4] {'head'}, dimensions={0}, use_global_device_ids=true | all-gather | bytes 819200 | tf_op jit(solution)/shard_map/all_gather | solution.py:55
  56.8 0.4 convolution_convert_fusion.3
  57.3 0.2 convolution_convert_fusion.1
  57.5 0.2 copy-done.3
  57.7 0.7 copy-done.7
  58.3 1.6 fusion.42
  59.9 0.0 reduce-scatter.9.cloned.1.call-update
  60.0 0.0 reduce-scatter.13.cloned.1.call-start
  60.0 0.2 convert_reduce_fusion
  60.2 0.3 fusion.2
  60.5 0.6 copy-done.14
  61.2 0.5 convolution_convert_fusion.2
  61.7 0.3 convolution_convert_fusion
  62.0 0.3 copy-done.4
  62.3 1.9 fusion.43
  64.1 0.0 reduce-scatter.13.cloned.1.call-update
  64.2 0.0 reduce-scatter.11.cloned.1.call-start
  64.2 0.8 copy-done.8
  65.1 2.0 fusion.35
  67.1 0.0 reduce-scatter.17.cloned.1.call-start
  67.1 3.9 fusion.23
  71.0 0.0 reduce-scatter.17.cloned.1.call-update
  71.1 0.0 reduce-scatter.15.cloned.1.call-start
  71.1 0.9 copy-done.11
  72.0 2.5 fusion.32
  74.6 0.1 convert_reduce_fusion.2
  74.7 0.2 fusion.22
  75.0 12.2 %reduce-scatter.9.cloned.1.call-done = f32[64,1280]{1,0:T(8,128)} async-done(((f32[256,1280]{1,0:T(8,128)}), f32[64,1280]{1,0:T(8,128)}) %reduce-scatter.9.cloned.1.call-update) | async-done | bytes 327696 | tf_op jit(solution)/shard_map/reduce_scatter | solution.py:69
  87.1 1.2 fusion.37
  88.4 1.8 fusion.21
  90.2 68.5 %reduce-scatter.13.cloned.1.call-done = f32[320,160]{0,1:T(8,128)} async-done(((f32[320,1280]{0,1:T(8,128)}), f32[320,160]{0,1:T(8,128)}) %reduce-scatter.13.cloned.1.call-update) | async-done | bytes 204816 | tf_op jit(solution)/shard_map/reduce_scatter | solution.py:77
  158.7 70.5 %reduce-scatter.11.cloned.1.call-done = f32[160,320]{1,0:T(8,128)} async-done(((f32[1280,320]{1,0:T(8,128)}), f32[160,320]{1,0:T(8,128)}) %reduce-scatter.11.cloned.1.call-update) | async-done | bytes 204816 | tf_op jit(solution)/shard_map/reduce_scatter | solution.py:81
  229.2 79.7 %reduce-scatter.17.cloned.1.call-done = f32[640,160]{0,1:T(8,128)} async-done(((f32[640,1280]{0,1:T(8,128)}), f32[640,160]{0,1:T(8,128)}) %reduce-scatter.17.cloned.1.call-update) | async-done | bytes 409616 | tf_op jit(solution)/shard_map/reduce_scatter | solution.py:76
  308.9 79.4 %reduce-scatter.15.cloned.1.call-done = f32[160,640]{1,0:T(8,128)} async-done(((f32[1280,640]{1,0:T(8,128)}), f32[160,640]{1,0:T(8,128)}) %reduce-scatter.15.cloned.1.call-update) | async-done | bytes 409616 | tf_op jit(solution)/shard_map/reduce_scatter | solution.py:80
  (37 shorter events, 0.2 us)
Async XLA Ops:
  7.2 5.1 %copy-start = (bf16[1280,640]{1,0:T(8,128)(2,1)S(1)}, bf16[1280,640]{1,0:T(8,128)(2,1)}, u32[]{:S(2)}) copy-start(bf16[1280,640]{1,0:T(8,128)(2,1)} %param.14) | copy-start | bytes 4915204
  7.2 2.9 copy-start.5
  7.2 38.8 %reduce-scatter.7.cloned.1.call-start = ((), (), s32[]{:S(2)}) async-start(), calls=%async_computation.6 | async-start | bytes 1638400 | tf_op jit(solution)/shard_map/reduce_scatter | solution.py:53
  10.1 2.2 copy-start.2
  14.1 0.7 copy-start.10
  16.7 70.5 %reduce-scatter.9.cloned.1.call-start = ((), (), s32[]{:S(2)}) async-start(), calls=%async_computation.7 | async-start | bytes 1638400 | tf_op jit(solution)/shard_map/reduce_scatter | solution.py:69
  46.0 10.8 %copy-start.12 = (bf16[320,1280]{1,0:T(8,128)(2,1)S(1)}, bf16[320,1280]{1,0:T(8,128)(2,1)}, u32[]{:S(2)}) copy-start(bf16[320,1280]{1,0:T(8,128)(2,1)} %param.13) | copy-start | bytes 2457604
  49.4 7.9 %copy-start.6 = (bf16[1,4,256,256]{3,2,1,0:T(8,128)(2,1)S(1)}, bf16[1,4,256,256]{3,2,1,0:T(8,128)(2,1)}, u32[]{:S(2)}) copy-start(bf16[1,4,256,256]{3,2,1,0:T(8,128)(2,1)} %param.11) | copy-start | bytes 1572868
  56.8 0.8 copy-start.3
  56.8 1.5 copy-start.13
  57.7 0.7 copy-start.7
  58.3 1.7 copy-start.1
  60.0 98.7 %reduce-scatter.13.cloned.1.call-start = ((), (), s32[]{:S(2)}) async-start(), calls=%async_computation.9 | async-start | bytes 2211840 | tf_op jit(solution)/shard_map/reduce_scatter | solution.py:77
  60.0 1.1 copy-start.14
  61.2 1.1 copy-start.4
  64.1 0.9 copy-start.8
  64.2 165.0 %reduce-scatter.11.cloned.1.call-start = ((), (), s32[]{:S(2)}) async-start(), calls=%async_computation.8 | async-start | bytes 2211840 | tf_op jit(solution)/shard_map/reduce_scatter | solution.py:81
  67.1 241.8 %reduce-scatter.17.cloned.1.call-start = ((), (), s32[]{:S(2)}) async-start(), calls=%async_computation.11 | async-start | bytes 3686400 | tf_op jit(solution)/shard_map/reduce_scatter | solution.py:76
  71.0 1.0 copy-start.11
  71.1 317.2 %reduce-scatter.15.cloned.1.call-start = ((), (), s32[]{:S(2)}) async-start(), calls=%async_computation.10 | async-start | bytes 3686400 | tf_op jit(solution)/shard_map/reduce_scatter | solution.py:80
  74.6 13.8 %copy-start.9 = (f32[64,1280]{1,0:T(8,128)S(1)}, f32[64,1280]{1,0:T(8,128)}, u32[]{:S(2)}) copy-start(f32[64,1280]{1,0:T(8,128)} %get-tuple-element.10) | copy-start | bytes 983044
Sparse Core Ops, SparseCore 0:
  16.8 29.1 reduce-scatter.6
  60.1 27.0 reduce-scatter.8
  91.2 67.4 reduce-scatter.12
  162.6 66.5 reduce-scatter.10
  233.2 75.5 reduce-scatter.16
  312.9 75.3 reduce-scatter.14
where the time goes:
time: 396 us; the launch traced here: 395 us
  waiting for transfers between devices  336 us (85%)
  matrix products  19.1 us (5%)
  between operations  14.3 us (4%)
  other arithmetic  13.5 us (3%)
  blocking collectives  7.45 us (2%)
  local copies, waits for them, and re-layouts  4.29 us (1%)
    reduce_scatter x1, waiting for transfers between devices, on_device(): lax.psum_scatter(down_term, 'img', scatter_dimension=1, tiled=True)  79.7 us
    reduce_scatter x1, waiting for transfers between devices, on_device(): lax.psum_scatter(up_term, 'img', scatter_dimension=0, tiled=True)  79.4 us
    reduce_scatter x1, waiting for transfers between devices, on_device(): lax.psum_scatter(value_term, 'img', scatter_dimension=0, tiled=True)  70.5 us
    reduce_scatter x1, waiting for transfers between devices, on_device(): lax.psum_scatter(outproj_term, 'img', scatter_dimension=1, tiled=True)  68.5 us
    reduce_scatter x1, waiting for transfers between devices, on_device(): lax.psum_scatter(mid_part, 'head', scatter_dimension=0, tiled=True)  25.8 us
    reduce_scatter x1, waiting for transfers between devices, on_device(): lax.psum_scatter(input_part, 'head', scatter_dimension=0, tiled=True)  12.2 us
  transfers between devices with their start and end apart: 6, of which 6 were waited for; matrix products, arithmetic and copies ran while one was open for 5% of the time, Pallas kernels for 0%

commit v1 on v0

--- a/solution.py
+++ b/solution.py
@@ -1,6 +1,8 @@
 import jax
 import jax.numpy as jnp
 from jax import lax
+from jax.experimental import pallas as pl
+from jax.experimental.pallas import tpu as pltpu
 from jax.sharding import PartitionSpec as P
 
 
@@ -83,9 +85,259 @@
     return (in_grad, grad_value, grad_out, grad_up, grad_down)
 
 
+MESH = pl.DeviceIdType.MESH
+F32 = jnp.float32
+BF16 = jnp.bfloat16
+GELU_C = 0.7978845608028654
+
+
+def dot_nn(a, b):
+    return lax.dot_general(a, b, (((1,), (0,)), ((), ())), preferred_element_type=F32)
+
+
+def dot_nt(a, b):
+    return lax.dot_general(a, b, (((1,), (1,)), ((), ())), preferred_element_type=F32)
+
+
+def dot_tn(a, b):
+    return lax.dot_general(a, b, (((0,), (0,)), ((), ())), preferred_element_type=F32)
+
+
+def gelu_and_slope(pre):
+    square = pre * pre
+    tanh = jnp.tanh(GELU_C * pre * (1.0 + 0.044715 * square))
+    half = 0.5 * (1.0 + tanh)
+    slope = half + 0.5 * pre * (1.0 - tanh * tanh) * (GELU_C * (1.0 + 3 * 0.044715 * square))
+    return pre * half, slope
+
+
+def block_kernel(
+    inputs, middle, out_grad, maps, w_value, w_out, w_up, w_down,
+    in_grad, value_rows, out_rows_t, up_rows, down_rows_t,
+    mid2, og2, nm, nin, hid, prg, attd, vgr, mp, rs1, rs2, midb, mid_own,
+    mlp_buf, att_buf, xr, xs, zr1, zr2, send_sem, recv_sem,
+):
+    tok, width = inputs.shape
+    share = tok // 4
+    half_rows = tok // 2
+    heads_here = maps.shape[0]
+    local = attd.shape[1]
+    hdim = local // heads_here
+    ff = hid.shape[2]
+    img = lax.axis_index("img")
+    head = lax.axis_index("head")
+    z = img // 2
+    x = img % 2
+    core = head % 2
+    x_peer = {"img": z * 2 + (1 - x)}
+    core_peer = {"head": head + 1 - 2 * core}
+    head_ids = [(head + p) % 4 for p in (1, 2, 3)]
+    z_ids = [(z + q) % 4 for q in (1, 2, 3)]
+
+    def copy(src, dst, sem, peer):
+        return pltpu.make_async_remote_copy(
+            src_ref=src, dst_ref=dst, send_sem=send_sem.at[sem], recv_sem=recv_sem.at[sem],
+            device_id=peer, device_id_type=MESH,
+        )
+
+    barrier = pltpu.get_barrier_semaphore()
+    for peer in [x_peer] + [{"head": h} for h in head_ids] + [{"img": k * 2 + x} for k in z_ids]:
+        pl.semaphore_signal(barrier, inc=1, device_id=peer, device_id_type=MESH)
+    pl.semaphore_wait(barrier, 7)
+
+    mine = pl.ds(pl.multiple_of(core * half_rows, half_rows), half_rows)
+    gather = [
+        copy(middle.at[mine], mid2.at[mine], 0, x_peer),
+        copy(out_grad.at[mine], og2.at[mine], 1, x_peer),
+    ]
+    for c in gather:
+        c.start()
+    forward = [
+        copy(mid2.at[mine], mid2.at[mine], 2, core_peer),
+        copy(og2.at[mine], og2.at[mine], 3, core_peer),
+    ]
+
+    def mlp(slot, rows, grad):
+        normed = norm_rows(rows[...].astype(F32)).astype(BF16)
+        nm[slot] = normed
+        pre = dot_nn(normed, w_up[...])
+        value, slope = gelu_and_slope(pre)
+        hid[slot] = value.astype(BF16)
+        prg[slot] = (slope * dot_nt(grad[...], w_down[...])).astype(BF16)
+
+    mlp(0, middle, out_grad)
+    mp[0] = dot_nt(prg[0], w_up[...]).astype(BF16)
+
+    def scatter(slot, landing, first_sem):
+        return [
+            copy(mp.at[slot, pl.ds(pl.multiple_of(h * share, share), share)], landing.at[p], first_sem + p, {"head": h})
+            for p, h in enumerate(head_ids)
+        ]
+
+    own = pl.ds(pl.multiple_of(head * share, share), share)
+    scatter1 = scatter(0, rs1, 4)
+    for c in scatter1:
+        c.start()
+
+    nin[...] = norm_rows(inputs[...].astype(F32)).astype(BF16)
+    values = dot_nn(nin[...], w_value[...]).astype(BF16)
+    column = lax.broadcasted_iota(jnp.int32, (tok, local), 1)
+
+    def own_columns(array, h):
+        keep = (column >= h * hdim) & (column < (h + 1) * hdim)
+        return jnp.where(keep, array, jnp.zeros_like(array))
+
+    total = dot_nn(maps[0], own_columns(values, 0))
+    for h in range(1, heads_here):
+        total = total + dot_nn(maps[h], own_columns(values, h))
+    attd[...] = total.astype(BF16)
+
+    for c in gather:
+        c.wait_recv()
+    for c in forward:
+        c.start()
+
+    for c in scatter1:
+        c.wait_recv()
+    grad_sum = mp[0, own].astype(F32) + rs1[0].astype(F32) + rs1[1].astype(F32) + rs1[2].astype(F32)
+    mid_rows = out_grad[own].astype(F32) + norm_back(middle[own].astype(F32), grad_sum)
+    mid_own[...] = mid_rows
+    midb[own] = mid_rows.astype(BF16)
+    spread = [copy(midb.at[own], midb.at[own], 7 + p, {"head": h}) for p, h in enumerate(head_ids)]
+    for c in spread:
+        c.start()
+
+    for c in forward:
+        c.wait_recv()
+    mlp(1, mid2, og2)
+
+    tile = 256
+
+    def mlp_terms(step, carry):
+        cols = pl.ds(pl.multiple_of(step * tile, tile), tile)
+        down = dot_tn(out_grad[:, cols], hid[0]) + dot_tn(og2[:, cols], hid[1])
+        up = dot_tn(nm[0, :, cols], prg[0]) + dot_tn(nm[1, :, cols], prg[1])
+        mlp_buf[cols, 0:ff] = down.astype(BF16)
+        mlp_buf[cols, ff:2 * ff] = up.astype(BF16)
+        return carry
+
+    lax.fori_loop(0, width // tile, mlp_terms, 0)
+    piece = up_rows.shape[0]
+
+    def chunk(at_z, at_x):
+        return pl.ds(pl.multiple_of((at_z * 2 + at_x) * piece, piece), piece)
+
+    z_mlp = [
+        copy(mlp_buf.at[chunk(k, x)], zr1.at[q], 10 + q, {"img": k * 2 + x}) for q, k in enumerate(z_ids)
+    ]
+    for c in z_mlp:
+        c.start()
+
+    for c in spread:
+        c.wait_recv()
+    att_grad = dot_nt(midb[...], w_out[...]).astype(BF16)
+    total = dot_tn(maps[0], own_columns(att_grad, 0))
+    for h in range(1, heads_here):
+        total = total + dot_tn(maps[h], own_columns(att_grad, h))
+    vgr[...] = total.astype(BF16)
+    mp[1] = dot_nt(vgr[...], w_value[...]).astype(BF16)
+    scatter2 = scatter(1, rs2, 13)
+    for c in scatter2:
+        c.start()
+
+    def att_terms(step, carry):
+        cols = pl.ds(pl.multiple_of(step * tile, tile), tile)
+        att_buf[cols, 0:local] = dot_tn(midb[:, cols], attd[...]).astype(BF16)
+        att_buf[cols, local:2 * local] = dot_tn(nin[:, cols], vgr[...]).astype(BF16)
+        return carry
+
+    lax.fori_loop(0, width // tile, att_terms, 0)
+    order = z_ids + [z]
+    x_att = [copy(att_buf.at[chunk(k, 1 - x)], xr.at[q], 16 + q, x_peer) for q, k in enumerate(order)]
+    for c in x_att:
+        c.start()
+
+    for c in scatter2:
+        c.wait_recv()
+    grad_sum = mp[1, own].astype(F32) + rs2[0].astype(F32) + rs2[1].astype(F32) + rs2[2].astype(F32)
+    in_grad[...] = (mid_own[...] + norm_back(inputs[own].astype(F32), grad_sum)).astype(BF16)
+
+    z_att = []
+    for q, k in enumerate(z_ids):
+        x_att[q].wait_recv()
+        xs[q] = (att_buf[chunk(k, x)].astype(F32) + xr[q].astype(F32)).astype(BF16)
+        c = copy(xs.at[q], zr2.at[q], 20 + q, {"img": k * 2 + x})
+        c.start()
+        z_att.append(c)
+    x_att[3].wait_recv()
+
+    for c in z_mlp:
+        c.wait_recv()
+    total = mlp_buf[chunk(z, x)].astype(F32) + zr1[0].astype(F32) + zr1[1].astype(F32) + zr1[2].astype(F32)
+    down_rows_t[...] = total[:, 0:ff]
+    up_rows[...] = total[:, ff:2 * ff]
+    for c in z_att:
+        c.wait_recv()
+    total = att_buf[chunk(z, x)].astype(F32) + xr[3].astype(F32)
+    total = total + zr2[0].astype(F32) + zr2[1].astype(F32) + zr2[2].astype(F32)
+    out_rows_t[...] = total[:, 0:local]
+    value_rows[...] = total[:, local:2 * local]
+    for c in gather + forward + scatter1 + spread + z_mlp + scatter2 + x_att + z_att:
+        c.wait_send()
+
+
+def on_device_fused(inputs, middle, out_grad, cached_maps, w_value, w_out, w_up, w_down):
+    tok, width = inputs.shape
+    local, ff = w_value.shape[1], w_up.shape[1]
+    piece = width // lax.axis_size("img")
+    share = tok // 4
+    vmem = pl.BlockSpec(memory_space=pltpu.VMEM)
+    shape = jax.ShapeDtypeStruct
+    in_grad, value_rows, out_rows_t, up_rows, down_rows_t = pl.pallas_call(
+        block_kernel,
+        out_shape=(
+            shape((share, width), BF16),
+            shape((piece, local), F32),
+            shape((piece, local), F32),
+            shape((piece, ff), F32),
+            shape((piece, ff), F32),
+        ),
+        in_specs=[vmem] * 8,
+        out_specs=(vmem,) * 5,
+        scratch_shapes=[
+            pltpu.VMEM((tok, width), BF16),
+            pltpu.VMEM((tok, width), BF16),
+            pltpu.VMEM((2, tok, width), BF16),
+            pltpu.VMEM((tok, width), BF16),
+            pltpu.VMEM((2, tok, ff), BF16),
+            pltpu.VMEM((2, tok, ff), BF16),
+            pltpu.VMEM((tok, local), BF16),
+            pltpu.VMEM((tok, local), BF16),
+            pltpu.VMEM((2, tok, width), BF16),
+            pltpu.VMEM((3, share, width), BF16),
+            pltpu.VMEM((3, share, width), BF16),
+            pltpu.VMEM((tok, width), BF16),
+            pltpu.VMEM((share, width), F32),
+            pltpu.VMEM((width, 2 * ff), BF16),
+            pltpu.VMEM((width, 2 * local), BF16),
+            pltpu.VMEM((4, piece, 2 * local), BF16),
+            pltpu.VMEM((3, piece, 2 * local), BF16),
+            pltpu.VMEM((3, piece, 2 * ff), BF16),
+            pltpu.VMEM((3, piece, 2 * local), BF16),
+            pltpu.SemaphoreType.DMA((23,)),
+            pltpu.SemaphoreType.DMA((23,)),
+        ],
+        compiler_params=pltpu.CompilerParams(
+            collective_id=0, has_side_effects=True, vmem_limit_bytes=56 * 1024 * 1024
+        ),
+    )(inputs, middle, out_grad, cached_maps[0], w_value, w_out, w_up, w_down)
+    return in_grad, value_rows, out_rows_t.T, up_rows, down_rows_t.T
+
+
 def solution(mesh):
+    fused = mesh.shape["img"] == 8 and mesh.shape["head"] == 4
     return jax.shard_map(
-        on_device,
+        on_device_fused if fused else on_device,
         mesh=mesh,
         in_specs=(
             P("img", None),

time: 396 us -> 95.2 us (0.24)
  the two profiles are of different devices: /device:TPU:0 before, /device:TPU:9 now
where the time goes in v1:
time: 95.2 us; the launch traced here: 94.9 us
  Pallas kernels  84.6 us (89%)
  local copies, waits for them, and re-layouts  9.71 us (10%)
    pallas_call x1, Pallas kernels, on_device_fused(): pl.pallas_call(block_kernel, out_shape=(shape((share, width), BF16), shap...  84.6 us
    unnamed x8, local copies, waits for them, and re-layouts  9.71 us

profile of v1, /device:TPU:9, one launch (start us, length us, event | category | flops | bytes accessed | tf_op | source)
XLA Modules:
  0.0 94.9 jit_solution(13257337198116060597)
XLA Ops:
  0.6 2.2 %copy.13.w_value = bf16[1280,320]{1,0:T(8,128)(2,1)} copy(bf16[1280,320]{0,1:T(8,128)(2,1)} %param.12) | data formatting | bytes 1638400 | tf_op args[4]
  2.9 84.6 %shard_map.119 = (bf16[64,1280]{1,0:T(8,128)(2,1)}, f32[160,320]{1,0:T(8,128)}, f32[160,320]{1,0:T(8,128)}, f32[160,640]{1,0:T(8,128)}, f32[160,640]{1,0:T(8,128)}) custom-call(bf16[256,1280]{1,0:T(8,128)(2,1)} %inputs.1, bf16[256,1280]{1,0:T(8,128)(2,1)} %middle.1, bf16[256,1280]{1,0:T(8,128)(2,1)} %out_grad.1, bf16[4,256,256]{2,1,0:T(8,128)(2,1)} %bitcast.3, ...), custom_call_target="tpu_custom_call" | custom-call | tf_op jit(solution)/shard_map/pallas_call | solution.py:296
  87.4 0.0 copy-start
  87.5 1.6 %copy.19 = bf16[64,1280]{1,0:T(8,128)(2,1)} copy(bf16[64,1280]{1,0:T(8,128)(2,1)} %get-tuple-element.20) | data formatting | bytes 327680
  89.1 1.7 %copy.20 = f32[160,320]{1,0:T(8,128)} copy(f32[160,320]{1,0:T(8,128)} %get-tuple-element.21) | data formatting | bytes 409600
  90.7 1.7 %copy.21 = f32[320,160]{0,1:T(8,128)} copy(f32[320,160]{0,1:T(8,128)} %bitcast.5) | data formatting | bytes 409600
  92.4 1.8 %copy.22 = f32[160,640]{1,0:T(8,128)} copy(f32[160,640]{1,0:T(8,128)} %get-tuple-element.23) | data formatting | bytes 819200
  94.2 0.0 copy-done
  94.2 0.8 copy.23
Async XLA Ops:
  87.4 6.7 %copy-start = (f32[160,640]{1,0:T(8,128)S(1)}, f32[160,640]{1,0:T(8,128)}, u32[]{:S(2)}) copy-start(f32[160,640]{1,0:T(8,128)} %get-tuple-element.14) | copy-start | bytes 1228804

commit v2 on v1

--- a/solution.py
+++ b/solution.py
@@ -112,27 +112,32 @@
 
 
 def block_kernel(
-    inputs, middle, out_grad, maps, w_value, w_out, w_up, w_down,
-    in_grad, value_rows, out_rows_t, up_rows, down_rows_t,
-    mid2, og2, nm, nin, hid, prg, attd, vgr, mp, rs1, rs2, midb, mid_own,
-    mlp_buf, att_buf, xr, xs, zr1, zr2, send_sem, recv_sem,
+    inputs_h, middle_h, out_grad_h, maps_h, w_value_h, w_out_h, w_up_h, w_down_h,
+    in_grad, mlp_sum, att_sum,
+    inputs, middle, out_grad, maps, w_value_t, w_out, w_up, w_down,
+    mid2, og2, nmt, ogt, nint, midbt, hid, prg, attd, vgr, mp, rs1, rs2, midb, mid_own,
+    mlp_buf, att_buf, xr, zr1, zs1, zr2, zs2, local_sem, send_sem, recv_sem,
 ):
     tok, width = inputs.shape
     share = tok // 4
-    half_rows = tok // 2
+    quarter = tok // 4
     heads_here = maps.shape[0]
     local = attd.shape[1]
     hdim = local // heads_here
     ff = hid.shape[2]
+    piece = mlp_sum.shape[0]
     img = lax.axis_index("img")
     head = lax.axis_index("head")
     z = img // 2
     x = img % 2
     core = head % 2
+    upper = z // 2
+    depth = z % 2 * (1 - 2 * upper) + upper
     x_peer = {"img": z * 2 + (1 - x)}
     core_peer = {"head": head + 1 - 2 * core}
+    side_peer = {"img": (z + 1 - 2 * (z % 2)) * 2 + x}
+    across_peer = {"img": (3 - z) * 2 + x}
     head_ids = [(head + p) % 4 for p in (1, 2, 3)]
-    z_ids = [(z + q) % 4 for q in (1, 2, 3)]
 
     def copy(src, dst, sem, peer):
         return pltpu.make_async_remote_copy(
@@ -141,30 +146,38 @@
         )
 
     barrier = pltpu.get_barrier_semaphore()
-    for peer in [x_peer] + [{"head": h} for h in head_ids] + [{"img": k * 2 + x} for k in z_ids]:
+    for peer in [x_peer, side_peer, across_peer] + [{"head": h} for h in head_ids]:
         pl.semaphore_signal(barrier, inc=1, device_id=peer, device_id_type=MESH)
-    pl.semaphore_wait(barrier, 7)
-
-    mine = pl.ds(pl.multiple_of(core * half_rows, half_rows), half_rows)
-    gather = [
-        copy(middle.at[mine], mid2.at[mine], 0, x_peer),
-        copy(out_grad.at[mine], og2.at[mine], 1, x_peer),
+    loads = [
+        pltpu.make_async_copy(src, dst, local_sem.at[i])
+        for i, (src, dst) in enumerate([
+            (middle_h, middle), (w_up_h, w_up), (out_grad_h, out_grad), (w_down_h, w_down),
+            (inputs_h, inputs), (w_value_h, w_value_t), (maps_h, maps), (w_out_h, w_out),
+        ])
     ]
+    for c in loads:
+        c.start()
+    pl.semaphore_wait(barrier, 6)
+
+    gather, forward = [], []
+    for part in range(2):
+        rows = pl.ds(pl.multiple_of((core * 2 + part) * quarter, quarter), quarter)
+        for i, (src, dst) in enumerate([(middle_h, mid2), (out_grad_h, og2)]):
+            gather.append(copy(src.at[rows], dst.at[rows], part * 2 + i, x_peer))
+            forward.append(copy(dst.at[rows], dst.at[rows], 4 + part * 2 + i, core_peer))
     for c in gather:
         c.start()
-    forward = [
-        copy(mid2.at[mine], mid2.at[mine], 2, core_peer),
-        copy(og2.at[mine], og2.at[mine], 3, core_peer),
-    ]
 
     def mlp(slot, rows, grad):
         normed = norm_rows(rows[...].astype(F32)).astype(BF16)
-        nm[slot] = normed
+        nmt[slot] = normed.T
         pre = dot_nn(normed, w_up[...])
         value, slope = gelu_and_slope(pre)
         hid[slot] = value.astype(BF16)
         prg[slot] = (slope * dot_nt(grad[...], w_down[...])).astype(BF16)
 
+    for c in loads[:4]:
+        c.wait()
     mlp(0, middle, out_grad)
     mp[0] = dot_nt(prg[0], w_up[...]).astype(BF16)
 
@@ -175,12 +188,16 @@
         ]
 
     own = pl.ds(pl.multiple_of(head * share, share), share)
-    scatter1 = scatter(0, rs1, 4)
+    scatter1 = scatter(0, rs1, 8)
     for c in scatter1:
         c.start()
 
-    nin[...] = norm_rows(inputs[...].astype(F32)).astype(BF16)
-    values = dot_nn(nin[...], w_value[...]).astype(BF16)
+    for c in loads[4:]:
+        c.wait()
+    ogt[0] = out_grad[...].T
+    normed_in = norm_rows(inputs[...].astype(F32)).astype(BF16)
+    nint[...] = normed_in.T
+    values = dot_nt(normed_in, w_value_t[...]).astype(BF16)
     column = lax.broadcasted_iota(jnp.int32, (tok, local), 1)
 
     def own_columns(array, h):
@@ -192,9 +209,8 @@
         total = total + dot_nn(maps[h], own_columns(values, h))
     attd[...] = total.astype(BF16)
 
-    for c in gather:
-        c.wait_recv()
-    for c in forward:
+    for got, c in zip(gather, forward):
+        got.wait_recv()
         c.start()
 
     for c in scatter1:
@@ -203,35 +219,40 @@
     mid_rows = out_grad[own].astype(F32) + norm_back(middle[own].astype(F32), grad_sum)
     mid_own[...] = mid_rows
     midb[own] = mid_rows.astype(BF16)
-    spread = [copy(midb.at[own], midb.at[own], 7 + p, {"head": h}) for p, h in enumerate(head_ids)]
+    spread = [copy(midb.at[own], midb.at[own], 11 + p, {"head": h}) for p, h in enumerate(head_ids)]
     for c in spread:
         c.start()
 
     for c in forward:
         c.wait_recv()
     mlp(1, mid2, og2)
-
-    tile = 256
-
-    def mlp_terms(step, carry):
-        cols = pl.ds(pl.multiple_of(step * tile, tile), tile)
-        down = dot_tn(out_grad[:, cols], hid[0]) + dot_tn(og2[:, cols], hid[1])
-        up = dot_tn(nm[0, :, cols], prg[0]) + dot_tn(nm[1, :, cols], prg[1])
-        mlp_buf[cols, 0:ff] = down.astype(BF16)
-        mlp_buf[cols, ff:2 * ff] = up.astype(BF16)
-        return carry
-
-    lax.fori_loop(0, width // tile, mlp_terms, 0)
-    piece = up_rows.shape[0]
-
-    def chunk(at_z, at_x):
-        return pl.ds(pl.multiple_of((at_z * 2 + at_x) * piece, piece), piece)
-
-    z_mlp = [
-        copy(mlp_buf.at[chunk(k, x)], zr1.at[q], 10 + q, {"img": k * 2 + x}) for q, k in enumerate(z_ids)
-    ]
-    for c in z_mlp:
-        c.start()
+    ogt[1] = og2[...].T
+
+    def actual(c):
+        return c * (1 - 2 * upper) + 3 * upper
+
+    def chunk(c, at_x):
+        return pl.ds(pl.multiple_of((actual(c) * 2 + at_x) * piece, piece), piece)
+
+    def exchange(buf, zr, zs, first_sem):
+        ends = [copy(buf.at[c], zr.at[i], first_sem + i, side_peer) for i, c in enumerate((3, 2, 1))]
+        cross = [copy(zs.at[i], zr.at[3 + i], first_sem + 3 + i, across_peer) for i in range(2)]
+        back = copy(zs.at[2], zr.at[5], first_sem + 5, side_peer)
+        return ends, cross, back
+
+    ends1, cross1, back1 = exchange(mlp_buf, zr1, zs1, 14)
+    ends2, cross2, back2 = exchange(att_buf, zr2, zs2, 20)
+
+    for i, c in enumerate((3, 2, 1, 0)):
+        rows = chunk(c, x)
+        down = dot_nn(ogt[0, rows], hid[0]) + dot_nn(ogt[1, rows], hid[1])
+        up = dot_nn(nmt[0, rows], prg[0]) + dot_nn(nmt[1, rows], prg[1])
+        mlp_buf[c, :, 0:ff] = down.astype(BF16)
+        mlp_buf[c, :, ff:2 * ff] = up.astype(BF16)
+        if i < 3:
+            @pl.when(depth == 0)
+            def _():
+                ends1[i].start()
 
     for c in spread:
         c.wait_recv()
@@ -240,61 +261,157 @@
     for h in range(1, heads_here):
         total = total + dot_tn(maps[h], own_columns(att_grad, h))
     vgr[...] = total.astype(BF16)
-    mp[1] = dot_nt(vgr[...], w_value[...]).astype(BF16)
-    scatter2 = scatter(1, rs2, 13)
+    mp[1] = dot_nn(vgr[...], w_value_t[...]).astype(BF16)
+    scatter2 = scatter(1, rs2, 26)
     for c in scatter2:
         c.start()
-
-    def att_terms(step, carry):
-        cols = pl.ds(pl.multiple_of(step * tile, tile), tile)
-        att_buf[cols, 0:local] = dot_tn(midb[:, cols], attd[...]).astype(BF16)
-        att_buf[cols, local:2 * local] = dot_tn(nin[:, cols], vgr[...]).astype(BF16)
-        return carry
-
-    lax.fori_loop(0, width // tile, att_terms, 0)
-    order = z_ids + [z]
-    x_att = [copy(att_buf.at[chunk(k, 1 - x)], xr.at[q], 16 + q, x_peer) for q, k in enumerate(order)]
-    for c in x_att:
-        c.start()
+    midbt[...] = midb[...].T
+
+    x_att = []
+    for to_peer in (True, False):
+        for i, c in enumerate((3, 2, 1, 0)):
+            rows = chunk(c, 1 - x if to_peer else x)
+            slot = 4 + c if to_peer else c
+            att_buf[slot, :, 0:local] = dot_nn(midbt[rows], attd[...]).astype(BF16)
+            att_buf[slot, :, local:2 * local] = dot_nn(nint[rows], vgr[...]).astype(BF16)
+            if to_peer:
+                x_att.append(copy(att_buf.at[slot], xr.at[c], 29 + c, x_peer))
+                x_att[i].start()
+
+    def add(buf, zs, zr, slot, c, i):
+        zs[slot] = (buf[c].astype(F32) + zr[i].astype(F32)).astype(BF16)
+
+    @pl.when(depth == 1)
+    def _():
+        ends1[0].wait_recv()
+        add(mlp_buf, zs1, zr1, 0, 3, 0)
+        cross1[0].start()
 
     for c in scatter2:
         c.wait_recv()
     grad_sum = mp[1, own].astype(F32) + rs2[0].astype(F32) + rs2[1].astype(F32) + rs2[2].astype(F32)
     in_grad[...] = (mid_own[...] + norm_back(inputs[own].astype(F32), grad_sum)).astype(BF16)
 
-    z_att = []
-    for q, k in enumerate(z_ids):
-        x_att[q].wait_recv()
-        xs[q] = (att_buf[chunk(k, x)].astype(F32) + xr[q].astype(F32)).astype(BF16)
-        c = copy(xs.at[q], zr2.at[q], 20 + q, {"img": k * 2 + x})
-        c.start()
-        z_att.append(c)
-    x_att[3].wait_recv()
-
-    for c in z_mlp:
-        c.wait_recv()
-    total = mlp_buf[chunk(z, x)].astype(F32) + zr1[0].astype(F32) + zr1[1].astype(F32) + zr1[2].astype(F32)
-    down_rows_t[...] = total[:, 0:ff]
-    up_rows[...] = total[:, ff:2 * ff]
-    for c in z_att:
-        c.wait_recv()
-    total = att_buf[chunk(z, x)].astype(F32) + xr[3].astype(F32)
-    total = total + zr2[0].astype(F32) + zr2[1].astype(F32) + zr2[2].astype(F32)
-    out_rows_t[...] = total[:, 0:local]
-    value_rows[...] = total[:, local:2 * local]
-    for c in gather + forward + scatter1 + spread + z_mlp + scatter2 + x_att + z_att:
+    @pl.when(depth == 1)
+    def _():
+        ends1[1].wait_recv()
+        add(mlp_buf, zs1, zr1, 1, 2, 1)
+        cross1[1].start()
+        cross1[0].wait_recv()
+        add(mlp_buf, zs1, zr1, 2, 0, 3)
+        back1.start()
+
+    for i, c in enumerate((3, 2, 1, 0)):
+        x_att[i].wait_recv()
+        att_buf[c] = (att_buf[c].astype(F32) + xr[c].astype(F32)).astype(BF16)
+        if i < 3:
+            @pl.when(depth == 0)
+            def _():
+                ends2[i].start()
+
+    @pl.when(depth == 1)
+    def _():
+        ends2[0].wait_recv()
+        add(att_buf, zs2, zr2, 0, 3, 0)
+        cross2[0].start()
+        ends2[1].wait_recv()
+        add(att_buf, zs2, zr2, 1, 2, 1)
+        cross2[1].start()
+        cross2[0].wait_recv()
+        add(att_buf, zs2, zr2, 2, 0, 3)
+        back2.start()
+        for ends, cross, back, buf, zr, result in (
+            (ends1, cross1, back1, mlp_buf, zr1, mlp_sum),
+            (ends2, cross2, back2, att_buf, zr2, att_sum),
+        ):
+            ends[2].wait_recv()
+            cross[1].wait_recv()
+            result[...] = buf[1].astype(F32) + zr[2].astype(F32) + zr[4].astype(F32)
+            for c in cross + [back]:
+                c.wait_send()
+
+    @pl.when(depth == 0)
+    def _():
+        for ends, back, buf, zr, result in (
+            (ends1, back1, mlp_buf, zr1, mlp_sum),
+            (ends2, back2, att_buf, zr2, att_sum),
+        ):
+            back.wait_recv()
+            result[...] = buf[0].astype(F32) + zr[5].astype(F32)
+            for c in ends:
+                c.wait_send()
+
+    for c in gather + forward + scatter1 + spread + scatter2 + x_att:
         c.wait_send()
+
+
+def split_kernel(in_grad, mlp_sum, att_sum, in_grad_out, value_rows, out_rows_t, up_rows, down_rows_t):
+    local, ff = value_rows.shape[1], up_rows.shape[1]
+    in_grad_out[...] = in_grad[...]
+    down_rows_t[...] = mlp_sum[:, 0:ff]
+    up_rows[...] = mlp_sum[:, ff:2 * ff]
+    out_rows_t[...] = att_sum[:, 0:local]
+    value_rows[...] = att_sum[:, local:2 * local]
 
 
 def on_device_fused(inputs, middle, out_grad, cached_maps, w_value, w_out, w_up, w_down):
     tok, width = inputs.shape
     local, ff = w_value.shape[1], w_up.shape[1]
+    heads_here = cached_maps.shape[1]
     piece = width // lax.axis_size("img")
     share = tok // 4
     vmem = pl.BlockSpec(memory_space=pltpu.VMEM)
     shape = jax.ShapeDtypeStruct
+    sums = pl.pallas_call(
+        block_kernel,
+        out_shape=(
+            shape((share, width), BF16),
+            shape((piece, 2 * ff), F32),
+            shape((piece, 2 * local), F32),
+        ),
+        in_specs=[pl.BlockSpec(memory_space=pl.ANY)] * 8,
+        out_specs=(vmem,) * 3,
+        scratch_shapes=[
+            pltpu.VMEM((tok, width), BF16),
+            pltpu.VMEM((tok, width), BF16),
+            pltpu.VMEM((tok, width), BF16),
+            pltpu.VMEM((heads_here, tok, tok), BF16),
+            pltpu.VMEM((local, width), BF16),
+            pltpu.VMEM((local, width), BF16),
+            pltpu.VMEM((width, ff), BF16),
+            pltpu.VMEM((ff, width), BF16),
+            pltpu.VMEM((tok, width), BF16),
+            pltpu.VMEM((tok, width), BF16),
+            pltpu.VMEM((2, width, tok), BF16),
+            pltpu.VMEM((2, width, tok), BF16),
+            pltpu.VMEM((width, tok), BF16),
+            pltpu.VMEM((width, tok), BF16),
+            pltpu.VMEM((2, tok, ff), BF16),
+            pltpu.VMEM((2, tok, ff), BF16),
+            pltpu.VMEM((tok, local), BF16),
+            pltpu.VMEM((tok, local), BF16),
+            pltpu.VMEM((2, tok, width), BF16),
+            pltpu.VMEM((3, share, width), BF16),
+            pltpu.VMEM((3, share, width), BF16),
+            pltpu.VMEM((tok, width), BF16),
+            pltpu.VMEM((share, width), F32),
+            pltpu.VMEM((4, piece, 2 * ff), BF16),
+            pltpu.VMEM((8, piece, 2 * local), BF16),
+            pltpu.VMEM((4, piece, 2 * local), BF16),
+            pltpu.VMEM((6, piece, 2 * ff), BF16),
+            pltpu.VMEM((3, piece, 2 * ff), BF16),
+            pltpu.VMEM((6, piece, 2 * local), BF16),
+            pltpu.VMEM((3, piece, 2 * local), BF16),
+            pltpu.SemaphoreType.DMA((8,)),
+            pltpu.SemaphoreType.DMA((33,)),
+            pltpu.SemaphoreType.DMA((33,)),
+        ],
+        compiler_params=pltpu.CompilerParams(
+            collective_id=0, has_side_effects=True, vmem_limit_bytes=56 * 1024 * 1024
+        ),
+    )(inputs, middle, out_grad, cached_maps[0], w_value.T, w_out, w_up, w_down)
     in_grad, value_rows, out_rows_t, up_rows, down_rows_t = pl.pallas_call(
-        block_kernel,
+        split_kernel,
         out_shape=(
             shape((share, width), BF16),
             shape((piece, local), F32),
@@ -302,35 +419,9 @@
             shape((piece, ff), F32),
             shape((piece, ff), F32),
         ),
-        in_specs=[vmem] * 8,
+        in_specs=[vmem] * 3,
         out_specs=(vmem,) * 5,
-        scratch_shapes=[
-            pltpu.VMEM((tok, width), BF16),
-            pltpu.VMEM((tok, width), BF16),
-            pltpu.VMEM((2, tok, width), BF16),
-            pltpu.VMEM((tok, width), BF16),
-            pltpu.VMEM((2, tok, ff), BF16),
-            pltpu.VMEM((2, tok, ff), BF16),
-            pltpu.VMEM((tok, local), BF16),
-            pltpu.VMEM((tok, local), BF16),
-            pltpu.VMEM((2, tok, width), BF16),
-            pltpu.VMEM((3, share, width), BF16),
-            pltpu.VMEM((3, share, width), BF16),
-            pltpu.VMEM((tok, width), BF16),
-            pltpu.VMEM((share, width), F32),
-            pltpu.VMEM((width, 2 * ff), BF16),
-            pltpu.VMEM((width, 2 * local), BF16),
-            pltpu.VMEM((4, piece, 2 * local), BF16),
-            pltpu.VMEM((3, piece, 2 * local), BF16),
-            pltpu.VMEM((3, piece, 2 * ff), BF16),
-            pltpu.VMEM((3, piece, 2 * local), BF16),
-            pltpu.SemaphoreType.DMA((23,)),
-            pltpu.SemaphoreType.DMA((23,)),
-        ],
-        compiler_params=pltpu.CompilerParams(
-            collective_id=0, has_side_effects=True, vmem_limit_bytes=56 * 1024 * 1024
-        ),
-    )(inputs, middle, out_grad, cached_maps[0], w_value, w_out, w_up, w_down)
+    )(*sums)
     return in_grad, value_rows, out_rows_t.T, up_rows, down_rows_t.T
 
 

time: 95.2 us -> 75.3 us (0.79)
  the two profiles are of different devices: /device:TPU:9 before, /device:TPU:0 now
where the time goes in v2:
time: 75.3 us; the launch traced here: 75.1 us
  Pallas kernels  74.5 us (99%)
    pallas_call x1, Pallas kernels, on_device_fused(): pl.pallas_call(block_kernel, out_shape=(shape((share, width), BF16), shap...  72 us
    pallas_call x1, Pallas kernels, on_device_fused(): pl.pallas_call(split_kernel, out_shape=(shape((share, width), BF16), shap...  2.47 us

profile of v2, /device:TPU:0, one launch (start us, length us, event | category | flops | bytes accessed | tf_op | source)
XLA Modules:
  0.0 75.1 jit_solution(12593411394083193865)
XLA Ops:
  0.6 72.0 %shard_map.119 = (bf16[64,1280]{1,0:T(8,128)(2,1)}, f32[160,1280]{1,0:T(8,128)}, f32[160,640]{1,0:T(8,128)}) custom-call(bf16[256,1280]{1,0:T(8,128)(2,1)} %inputs_h.1, bf16[256,1280]{1,0:T(8,128)(2,1)} %middle_h.1, bf16[256,1280]{1,0:T(8,128)(2,1)} %out_grad_h.1, bf16[4,256,256]{2,1,0:T(8,128)(2,1)} %bitcast.5, bf16[320,1280]{1,0:T(8,128)(2,1)} %bitcast.4, ...), custom_call_target="tpu_custom_call" | custom-call | tf_op jit(solution)/shard_map/pallas_call | solution.py:365
  72.7 2.5 %shard_map.120 = (bf16[64,1280]{1,0:T(8,128)(2,1)}, f32[160,320]{1,0:T(8,128)}, f32[160,320]{1,0:T(8,128)}, f32[160,640]{1,0:T(8,128)}, f32[160,640]{1,0:T(8,128)}) custom-call(bf16[64,1280]{1,0:T(8,128)(2,1)} %get-tuple-element.13.in_grad, f32[160,1280]{1,0:T(8,128)} %get-tuple-element.14.mlp_sum, f32[160,640]{1,0:T(8,128)} %get-tuple-element.15.att_sum), custom_call_target="tpu_custom_call" | custom-call | tf_op jit(solution)/shard_map/pallas_call | solution.py:413

commit v3 on v2

--- a/solution.py
+++ b/solution.py
@@ -88,6 +88,7 @@
 MESH = pl.DeviceIdType.MESH
 F32 = jnp.float32
 BF16 = jnp.bfloat16
+EARLY = 128
 GELU_C = 0.7978845608028654
 
 
@@ -115,26 +116,26 @@
     inputs_h, middle_h, out_grad_h, maps_h, w_value_h, w_out_h, w_up_h, w_down_h,
     in_grad, mlp_sum, att_sum,
     inputs, middle, out_grad, maps, w_value_t, w_out, w_up, w_down,
-    mid2, og2, nmt, ogt, nint, midbt, hid, prg, attd, vgr, mp, rs1, rs2, midb, mid_own,
-    mlp_buf, att_buf, xr, zr1, zs1, zr2, zs2, local_sem, send_sem, recv_sem,
+    nmt, ogt, nint, midbt, hid, prg, attd, vgr, mp, rs1, rs2, midb, mid_own,
+    a_buf, b_buf, att_buf, xr_a, xr_b, xr, zr_a, zs_a, zr_b, zs_b, zr2, zs2, xs_a,
+    local_sem, send_sem, recv_sem,
 ):
     tok, width = inputs.shape
     share = tok // 4
-    quarter = tok // 4
     heads_here = maps.shape[0]
     local = attd.shape[1]
     hdim = local // heads_here
-    ff = hid.shape[2]
+    ff = hid.shape[1]
+    early = a_buf.shape[2] // 2
+    late = ff - early
     piece = mlp_sum.shape[0]
     img = lax.axis_index("img")
     head = lax.axis_index("head")
     z = img // 2
     x = img % 2
-    core = head % 2
     upper = z // 2
     depth = z % 2 * (1 - 2 * upper) + upper
     x_peer = {"img": z * 2 + (1 - x)}
-    core_peer = {"head": head + 1 - 2 * core}
     side_peer = {"img": (z + 1 - 2 * (z % 2)) * 2 + x}
     across_peer = {"img": (3 - z) * 2 + x}
     head_ids = [(head + p) % 4 for p in (1, 2, 3)]
@@ -159,27 +160,14 @@
         c.start()
     pl.semaphore_wait(barrier, 6)
 
-    gather, forward = [], []
-    for part in range(2):
-        rows = pl.ds(pl.multiple_of((core * 2 + part) * quarter, quarter), quarter)
-        for i, (src, dst) in enumerate([(middle_h, mid2), (out_grad_h, og2)]):
-            gather.append(copy(src.at[rows], dst.at[rows], part * 2 + i, x_peer))
-            forward.append(copy(dst.at[rows], dst.at[rows], 4 + part * 2 + i, core_peer))
-    for c in gather:
-        c.start()
-
-    def mlp(slot, rows, grad):
-        normed = norm_rows(rows[...].astype(F32)).astype(BF16)
-        nmt[slot] = normed.T
-        pre = dot_nn(normed, w_up[...])
-        value, slope = gelu_and_slope(pre)
-        hid[slot] = value.astype(BF16)
-        prg[slot] = (slope * dot_nt(grad[...], w_down[...])).astype(BF16)
-
     for c in loads[:4]:
         c.wait()
-    mlp(0, middle, out_grad)
-    mp[0] = dot_nt(prg[0], w_up[...]).astype(BF16)
+    normed = norm_rows(middle[...].astype(F32)).astype(BF16)
+    pre = dot_nn(normed, w_up[...])
+    value, slope = gelu_and_slope(pre)
+    hid[...] = value.astype(BF16)
+    prg[...] = (slope * dot_nt(out_grad[...], w_down[...])).astype(BF16)
+    mp[0] = dot_nt(prg[...], w_up[...]).astype(BF16)
 
     def scatter(slot, landing, first_sem):
         return [
@@ -188,13 +176,57 @@
         ]
 
     own = pl.ds(pl.multiple_of(head * share, share), share)
-    scatter1 = scatter(0, rs1, 8)
+    scatter1 = scatter(0, rs1, 0)
     for c in scatter1:
         c.start()
+    nmt[...] = normed.T
+    ogt[...] = out_grad[...].T
+
+    def actual(c):
+        return c * (1 - 2 * upper) + 3 * upper
+
+    def chunk(c, at_x):
+        return pl.ds(pl.multiple_of((actual(c) * 2 + at_x) * piece, piece), piece)
+
+    def exchange(buf, zr, zs, first_sem):
+        ends = [copy(buf.at[c], zr.at[i], first_sem + i, side_peer) for i, c in enumerate((3, 2, 1))]
+        cross = [copy(zs.at[i], zr.at[3 + i], first_sem + 3 + i, across_peer) for i in range(2)]
+        back = copy(zs.at[2], zr.at[5], first_sem + 5, side_peer)
+        return ends, cross, back
+
+    ends_a, cross_a, back_a = exchange(a_buf, zr_a, zs_a, 18)
+    ends_b, cross_b, back_b = exchange(b_buf, zr_b, zs_b, 24)
+    ends2, cross2, back2 = exchange(att_buf, zr2, zs2, 30)
+
+    def at_end(start):
+        @pl.when(depth == 0)
+        def _():
+            start()
+
+    def add(buf, zs, zr, slot, c, i):
+        zs[slot] = (buf[c].astype(F32) + zr[i].astype(F32)).astype(BF16)
+
+    order = (3, 2, 1 - depth, depth)
+    x_b = []
+    for i, c in enumerate(order):
+        rows = chunk(c, 1 - x)
+        b_buf[4 + c, :, 0:late] = dot_nn(ogt[rows], hid[:, early:ff]).astype(BF16)
+        b_buf[4 + c, :, late:2 * late] = dot_nn(nmt[rows], prg[:, early:ff]).astype(BF16)
+        x_b.append(copy(b_buf.at[4 + c], xr_b.at[i], 9 + i, x_peer))
+        x_b[i].start()
+        c = 3 - i
+        rows = pl.ds(pl.multiple_of(actual(c) * 2 * piece, piece), 2 * piece)
+        a_buf[c, :, 0:early] = dot_nn(ogt[rows], hid[:, 0:early]).astype(BF16)
+        a_buf[c, :, early:2 * early] = dot_nn(nmt[rows], prg[:, 0:early]).astype(BF16)
+        if i < 3:
+            at_end(ends_a[i].start)
+    for c in (3, 2, 1, 0):
+        rows = chunk(c, x)
+        b_buf[c, :, 0:late] = dot_nn(ogt[rows], hid[:, early:ff]).astype(BF16)
+        b_buf[c, :, late:2 * late] = dot_nn(nmt[rows], prg[:, early:ff]).astype(BF16)
 
     for c in loads[4:]:
         c.wait()
-    ogt[0] = out_grad[...].T
     normed_in = norm_rows(inputs[...].astype(F32)).astype(BF16)
     nint[...] = normed_in.T
     values = dot_nt(normed_in, w_value_t[...]).astype(BF16)
@@ -209,9 +241,19 @@
         total = total + dot_nn(maps[h], own_columns(values, h))
     attd[...] = total.astype(BF16)
 
-    for got, c in zip(gather, forward):
-        got.wait_recv()
-        c.start()
+    def pass_on(buf, zr, zs, ends, cross, i):
+        ends[i].wait_recv()
+        add(buf, zs, zr, i, 3 - i, i)
+        cross[i].start()
+
+    def give_back(buf, zr, zs, cross, back):
+        cross[0].wait_recv()
+        add(buf, zs, zr, 2, 0, 3)
+        back.start()
+
+    @pl.when(depth == 1)
+    def _():
+        pass_on(a_buf, zr_a, zs_a, ends_a, cross_a, 0)
 
     for c in scatter1:
         c.wait_recv()
@@ -219,40 +261,48 @@
     mid_rows = out_grad[own].astype(F32) + norm_back(middle[own].astype(F32), grad_sum)
     mid_own[...] = mid_rows
     midb[own] = mid_rows.astype(BF16)
-    spread = [copy(midb.at[own], midb.at[own], 11 + p, {"head": h}) for p, h in enumerate(head_ids)]
+    spread = [copy(midb.at[own], midb.at[own], 3 + p, {"head": h}) for p, h in enumerate(head_ids)]
     for c in spread:
         c.start()
 
-    for c in forward:
-        c.wait_recv()
-    mlp(1, mid2, og2)
-    ogt[1] = og2[...].T
-
-    def actual(c):
-        return c * (1 - 2 * upper) + 3 * upper
-
-    def chunk(c, at_x):
-        return pl.ds(pl.multiple_of((actual(c) * 2 + at_x) * piece, piece), piece)
-
-    def exchange(buf, zr, zs, first_sem):
-        ends = [copy(buf.at[c], zr.at[i], first_sem + i, side_peer) for i, c in enumerate((3, 2, 1))]
-        cross = [copy(zs.at[i], zr.at[3 + i], first_sem + 3 + i, across_peer) for i in range(2)]
-        back = copy(zs.at[2], zr.at[5], first_sem + 5, side_peer)
-        return ends, cross, back
-
-    ends1, cross1, back1 = exchange(mlp_buf, zr1, zs1, 14)
-    ends2, cross2, back2 = exchange(att_buf, zr2, zs2, 20)
-
-    for i, c in enumerate((3, 2, 1, 0)):
-        rows = chunk(c, x)
-        down = dot_nn(ogt[0, rows], hid[0]) + dot_nn(ogt[1, rows], hid[1])
-        up = dot_nn(nmt[0, rows], prg[0]) + dot_nn(nmt[1, rows], prg[1])
-        mlp_buf[c, :, 0:ff] = down.astype(BF16)
-        mlp_buf[c, :, ff:2 * ff] = up.astype(BF16)
+    def settle_b(i):
+        c = order[i]
+        x_b[i].wait_recv()
+        b_buf[c] = (b_buf[c].astype(F32) + xr_b[i].astype(F32)).astype(BF16)
         if i < 3:
-            @pl.when(depth == 0)
-            def _():
-                ends1[i].start()
+            at_end(ends_b[i].start)
+
+    settle_b(0)
+
+    @pl.when(depth == 1)
+    def _():
+        pass_on(a_buf, zr_a, zs_a, ends_a, cross_a, 1)
+        give_back(a_buf, zr_a, zs_a, cross_a, back_a)
+
+    x_a = copy(xs_a.at[1 - x], xr_a, 13, x_peer)
+
+    def split_a(total):
+        xs_a[0] = total[0:piece].astype(BF16)
+        xs_a[1] = total[piece:2 * piece].astype(BF16)
+
+    @pl.when(depth == 1)
+    def _():
+        ends_a[2].wait_recv()
+        cross_a[1].wait_recv()
+        split_a(a_buf[1].astype(F32) + zr_a[2].astype(F32) + zr_a[4].astype(F32))
+        x_a.start()
+
+    @pl.when(depth == 0)
+    def _():
+        back_a.wait_recv()
+        split_a(a_buf[0].astype(F32) + zr_a[5].astype(F32))
+        x_a.start()
+
+    settle_b(1)
+
+    @pl.when(depth == 1)
+    def _():
+        pass_on(b_buf, zr_b, zs_b, ends_b, cross_b, 0)
 
     for c in spread:
         c.wait_recv()
@@ -261,87 +311,89 @@
     for h in range(1, heads_here):
         total = total + dot_tn(maps[h], own_columns(att_grad, h))
     vgr[...] = total.astype(BF16)
+    midbt[...] = midb[...].T
+
+    x_att = []
+    for i, c in enumerate(order):
+        rows = chunk(c, 1 - x)
+        att_buf[4 + c, :, 0:local] = dot_nn(midbt[rows], attd[...]).astype(BF16)
+        att_buf[4 + c, :, local:2 * local] = dot_nn(nint[rows], vgr[...]).astype(BF16)
+        x_att.append(copy(att_buf.at[4 + c], xr.at[i], 14 + i, x_peer))
+        x_att[i].start()
     mp[1] = dot_nn(vgr[...], w_value_t[...]).astype(BF16)
-    scatter2 = scatter(1, rs2, 26)
+    scatter2 = scatter(1, rs2, 6)
     for c in scatter2:
         c.start()
-    midbt[...] = midb[...].T
-
-    x_att = []
-    for to_peer in (True, False):
-        for i, c in enumerate((3, 2, 1, 0)):
-            rows = chunk(c, 1 - x if to_peer else x)
-            slot = 4 + c if to_peer else c
-            att_buf[slot, :, 0:local] = dot_nn(midbt[rows], attd[...]).astype(BF16)
-            att_buf[slot, :, local:2 * local] = dot_nn(nint[rows], vgr[...]).astype(BF16)
-            if to_peer:
-                x_att.append(copy(att_buf.at[slot], xr.at[c], 29 + c, x_peer))
-                x_att[i].start()
-
-    def add(buf, zs, zr, slot, c, i):
-        zs[slot] = (buf[c].astype(F32) + zr[i].astype(F32)).astype(BF16)
-
-    @pl.when(depth == 1)
-    def _():
-        ends1[0].wait_recv()
-        add(mlp_buf, zs1, zr1, 0, 3, 0)
-        cross1[0].start()
-
+    settle_b(2)
+
+    @pl.when(depth == 1)
+    def _():
+        pass_on(b_buf, zr_b, zs_b, ends_b, cross_b, 1)
+        give_back(b_buf, zr_b, zs_b, cross_b, back_b)
+
+    for c in (3, 2, 1, 0):
+        rows = chunk(c, x)
+        att_buf[c, :, 0:local] = dot_nn(midbt[rows], attd[...]).astype(BF16)
+        att_buf[c, :, local:2 * local] = dot_nn(nint[rows], vgr[...]).astype(BF16)
+
+    settle_b(3)
+
+    def settle_att(i):
+        c = order[i]
+        x_att[i].wait_recv()
+        att_buf[c] = (att_buf[c].astype(F32) + xr[i].astype(F32)).astype(BF16)
+        if i < 3:
+            at_end(ends2[i].start)
+
+    settle_att(0)
     for c in scatter2:
         c.wait_recv()
     grad_sum = mp[1, own].astype(F32) + rs2[0].astype(F32) + rs2[1].astype(F32) + rs2[2].astype(F32)
     in_grad[...] = (mid_own[...] + norm_back(inputs[own].astype(F32), grad_sum)).astype(BF16)
-
-    @pl.when(depth == 1)
-    def _():
-        ends1[1].wait_recv()
-        add(mlp_buf, zs1, zr1, 1, 2, 1)
-        cross1[1].start()
-        cross1[0].wait_recv()
-        add(mlp_buf, zs1, zr1, 2, 0, 3)
-        back1.start()
-
-    for i, c in enumerate((3, 2, 1, 0)):
-        x_att[i].wait_recv()
-        att_buf[c] = (att_buf[c].astype(F32) + xr[c].astype(F32)).astype(BF16)
-        if i < 3:
-            @pl.when(depth == 0)
-            def _():
-                ends2[i].start()
-
-    @pl.when(depth == 1)
-    def _():
-        ends2[0].wait_recv()
-        add(att_buf, zs2, zr2, 0, 3, 0)
-        cross2[0].start()
-        ends2[1].wait_recv()
-        add(att_buf, zs2, zr2, 1, 2, 1)
-        cross2[1].start()
-        cross2[0].wait_recv()
-        add(att_buf, zs2, zr2, 2, 0, 3)
-        back2.start()
-        for ends, cross, back, buf, zr, result in (
-            (ends1, cross1, back1, mlp_buf, zr1, mlp_sum),
-            (ends2, cross2, back2, att_buf, zr2, att_sum),
-        ):
-            ends[2].wait_recv()
-            cross[1].wait_recv()
-            result[...] = buf[1].astype(F32) + zr[2].astype(F32) + zr[4].astype(F32)
-            for c in cross + [back]:
-                c.wait_send()
+    x_a.wait_recv()
+    total = xs_a[x].astype(F32) + xr_a[...].astype(F32)
+    mlp_sum[:, 0:early] = total[:, 0:early]
+    mlp_sum[:, ff:ff + early] = total[:, early:2 * early]
+    settle_att(1)
+
+    @pl.when(depth == 1)
+    def _():
+        pass_on(att_buf, zr2, zs2, ends2, cross2, 0)
+
+    settle_att(2)
+
+    @pl.when(depth == 1)
+    def _():
+        pass_on(att_buf, zr2, zs2, ends2, cross2, 1)
+        give_back(att_buf, zr2, zs2, cross2, back2)
+
+    settle_att(3)
+
+    def put_b(total):
+        mlp_sum[:, early:ff] = total[:, 0:late]
+        mlp_sum[:, ff + early:2 * ff] = total[:, late:2 * late]
+
+    @pl.when(depth == 1)
+    def _():
+        ends_b[2].wait_recv()
+        cross_b[1].wait_recv()
+        put_b(b_buf[1].astype(F32) + zr_b[2].astype(F32) + zr_b[4].astype(F32))
+        ends2[2].wait_recv()
+        cross2[1].wait_recv()
+        att_sum[...] = att_buf[1].astype(F32) + zr2[2].astype(F32) + zr2[4].astype(F32)
+        for c in cross_a + [back_a] + cross_b + [back_b] + cross2 + [back2]:
+            c.wait_send()
 
     @pl.when(depth == 0)
     def _():
-        for ends, back, buf, zr, result in (
-            (ends1, back1, mlp_buf, zr1, mlp_sum),
-            (ends2, back2, att_buf, zr2, att_sum),
-        ):
-            back.wait_recv()
-            result[...] = buf[0].astype(F32) + zr[5].astype(F32)
-            for c in ends:
-                c.wait_send()
-
-    for c in gather + forward + scatter1 + spread + scatter2 + x_att:
+        back_b.wait_recv()
+        put_b(b_buf[0].astype(F32) + zr_b[5].astype(F32))
+        back2.wait_recv()
+        att_sum[...] = att_buf[0].astype(F32) + zr2[5].astype(F32)
+        for c in ends_a + ends_b + ends2:
+            c.wait_send()
+
+    for c in scatter1 + spread + scatter2 + x_b + [x_a] + x_att:
         c.wait_send()
 
 
@@ -360,6 +412,7 @@
     heads_here = cached_maps.shape[1]
     piece = width // lax.axis_size("img")
     share = tok // 4
+    late = ff - EARLY
     vmem = pl.BlockSpec(memory_space=pltpu.VMEM)
     shape = jax.ShapeDtypeStruct
     sums = pl.pallas_call(
@@ -380,14 +433,12 @@
             pltpu.VMEM((local, width), BF16),
             pltpu.VMEM((width, ff), BF16),
             pltpu.VMEM((ff, width), BF16),
-            pltpu.VMEM((tok, width), BF16),
-            pltpu.VMEM((tok, width), BF16),
-            pltpu.VMEM((2, width, tok), BF16),
-            pltpu.VMEM((2, width, tok), BF16),
             pltpu.VMEM((width, tok), BF16),
             pltpu.VMEM((width, tok), BF16),
-            pltpu.VMEM((2, tok, ff), BF16),
-            pltpu.VMEM((2, tok, ff), BF16),
+            pltpu.VMEM((width, tok), BF16),
+            pltpu.VMEM((width, tok), BF16),
+            pltpu.VMEM((tok, ff), BF16),
+            pltpu.VMEM((tok, ff), BF16),
             pltpu.VMEM((tok, local), BF16),
             pltpu.VMEM((tok, local), BF16),
             pltpu.VMEM((2, tok, width), BF16),
@@ -395,16 +446,22 @@
             pltpu.VMEM((3, share, width), BF16),
             pltpu.VMEM((tok, width), BF16),
             pltpu.VMEM((share, width), F32),
-            pltpu.VMEM((4, piece, 2 * ff), BF16),
+            pltpu.VMEM((4, 2 * piece, 2 * EARLY), BF16),
+            pltpu.VMEM((8, piece, 2 * late), BF16),
             pltpu.VMEM((8, piece, 2 * local), BF16),
+            pltpu.VMEM((piece, 2 * EARLY), BF16),
+            pltpu.VMEM((4, piece, 2 * late), BF16),
             pltpu.VMEM((4, piece, 2 * local), BF16),
-            pltpu.VMEM((6, piece, 2 * ff), BF16),
-            pltpu.VMEM((3, piece, 2 * ff), BF16),
+            pltpu.VMEM((6, 2 * piece, 2 * EARLY), BF16),
+            pltpu.VMEM((3, 2 * piece, 2 * EARLY), BF16),
+            pltpu.VMEM((6, piece, 2 * late), BF16),
+            pltpu.VMEM((3, piece, 2 * late), BF16),
             pltpu.VMEM((6, piece, 2 * local), BF16),
             pltpu.VMEM((3, piece, 2 * local), BF16),
+            pltpu.VMEM((2, piece, 2 * EARLY), BF16),
             pltpu.SemaphoreType.DMA((8,)),
-            pltpu.SemaphoreType.DMA((33,)),
-            pltpu.SemaphoreType.DMA((33,)),
+            pltpu.SemaphoreType.DMA((36,)),
+            pltpu.SemaphoreType.DMA((36,)),
         ],
         compiler_params=pltpu.CompilerParams(
             collective_id=0, has_side_effects=True, vmem_limit_bytes=56 * 1024 * 1024

time: 75.3 us -> 65.8 us (0.87)
  Pallas kernels: 74.5 us -> 65 us
    pallas_call x1, Pallas kernels: 72 us -> 62.5 us  [on_device_fused(): pl.pallas_call(block_kernel, out_shape=(shape((share, width), BF16), shap...]
where the time goes in v3:
time: 65.8 us; the launch traced here: 65.6 us
  Pallas kernels  65 us (99%)
    pallas_call x1, Pallas kernels, on_device_fused(): pl.pallas_call(block_kernel, out_shape=(shape((share, width), BF16), shap...  62.5 us
    pallas_call x1, Pallas kernels, on_device_fused(): pl.pallas_call(split_kernel, out_shape=(shape((share, width), BF16), shap...  2.47 us

profile of v3, /device:TPU:0, one launch (start us, length us, event | category | flops | bytes accessed | tf_op | source)
XLA Modules:
  0.0 65.6 jit_solution(7996302414345272349)
XLA Ops:
  0.6 62.5 %shard_map.119 = (bf16[64,1280]{1,0:T(8,128)(2,1)}, f32[160,1280]{1,0:T(8,128)}, f32[160,640]{1,0:T(8,128)}) custom-call(bf16[256,1280]{1,0:T(8,128)(2,1)} %inputs_h.1, bf16[256,1280]{1,0:T(8,128)(2,1)} %middle_h.1, bf16[256,1280]{1,0:T(8,128)(2,1)} %out_grad_h.1, bf16[4,256,256]{2,1,0:T(8,128)(2,1)} %bitcast.5, bf16[320,1280]{1,0:T(8,128)(2,1)} %bitcast.4, ...), custom_call_target="tpu_custom_call" | custom-call | tf_op jit(solution)/shard_map/pallas_call | solution.py:418
  63.2 2.5 %shard_map.120 = (bf16[64,1280]{1,0:T(8,128)(2,1)}, f32[160,320]{1,0:T(8,128)}, f32[160,320]{1,0:T(8,128)}, f32[160,640]{1,0:T(8,128)}, f32[160,640]{1,0:T(8,128)}) custom-call(bf16[64,1280]{1,0:T(8,128)(2,1)} %get-tuple-element.13.in_grad, f32[160,1280]{1,0:T(8,128)} %get-tuple-element.14.mlp_sum, f32[160,640]{1,0:T(8,128)} %get-tuple-element.15.att_sum), custom_call_target="tpu_custom_call" | custom-call | tf_op jit(solution)/shard_map/pallas_call | solution.py:470

commit v4 on v3

--- a/solution.py
+++ b/solution.py
@@ -158,16 +158,17 @@
     ]
     for c in loads:
         c.start()
-    pl.semaphore_wait(barrier, 6)
-
-    for c in loads[:4]:
-        c.wait()
+    loads[0].wait()
     normed = norm_rows(middle[...].astype(F32)).astype(BF16)
+    nmt[...] = normed.T
+    loads[2].wait()
+    ogt[...] = out_grad[...].T
+    loads[1].wait()
     pre = dot_nn(normed, w_up[...])
     value, slope = gelu_and_slope(pre)
     hid[...] = value.astype(BF16)
+    loads[3].wait()
     prg[...] = (slope * dot_nt(out_grad[...], w_down[...])).astype(BF16)
-    mp[0] = dot_nt(prg[...], w_up[...]).astype(BF16)
 
     def scatter(slot, landing, first_sem):
         return [
@@ -176,11 +177,6 @@
         ]
 
     own = pl.ds(pl.multiple_of(head * share, share), share)
-    scatter1 = scatter(0, rs1, 0)
-    for c in scatter1:
-        c.start()
-    nmt[...] = normed.T
-    ogt[...] = out_grad[...].T
 
     def actual(c):
         return c * (1 - 2 * upper) + 3 * upper
@@ -206,6 +202,7 @@
     def add(buf, zs, zr, slot, c, i):
         zs[slot] = (buf[c].astype(F32) + zr[i].astype(F32)).astype(BF16)
 
+    pl.semaphore_wait(barrier, 6)
     order = (3, 2, 1 - depth, depth)
     x_b = []
     for i, c in enumerate(order):
@@ -220,6 +217,11 @@
         a_buf[c, :, early:2 * early] = dot_nn(nmt[rows], prg[:, 0:early]).astype(BF16)
         if i < 3:
             at_end(ends_a[i].start)
+        if i == 0:
+            mp[0] = dot_nt(prg[...], w_up[...]).astype(BF16)
+            scatter1 = scatter(0, rs1, 0)
+            for k in scatter1:
+                k.start()
     for c in (3, 2, 1, 0):
         rows = chunk(c, x)
         b_buf[c, :, 0:late] = dot_nn(ogt[rows], hid[:, early:ff]).astype(BF16)

time: 65.8 us -> 64.9 us (0.986)
  Pallas kernels: 65 us -> 64.1 us
    pallas_call x1, Pallas kernels: 62.5 us -> 61.6 us  [on_device_fused(): pl.pallas_call(block_kernel, out_shape=(shape((share, width), BF16), shap...]
where the time goes in v4:
time: 64.9 us; the launch traced here: 64.8 us
  Pallas kernels  64.1 us (99%)
    pallas_call x1, Pallas kernels, on_device_fused(): pl.pallas_call(block_kernel, out_shape=(shape((share, width), BF16), shap...  61.6 us
    pallas_call x1, Pallas kernels, on_device_fused(): pl.pallas_call(split_kernel, out_shape=(shape((share, width), BF16), shap...  2.47 us

profile of v4, /device:TPU:0, one launch (start us, length us, event | category | flops | bytes accessed | tf_op | source)
XLA Modules:
  0.0 64.8 jit_solution(10577986330345828256)
XLA Ops:
  0.6 61.6 %shard_map.119 = (bf16[64,1280]{1,0:T(8,128)(2,1)}, f32[160,1280]{1,0:T(8,128)}, f32[160,640]{1,0:T(8,128)}) custom-call(bf16[256,1280]{1,0:T(8,128)(2,1)} %inputs_h.1, bf16[256,1280]{1,0:T(8,128)(2,1)} %middle_h.1, bf16[256,1280]{1,0:T(8,128)(2,1)} %out_grad_h.1, bf16[4,256,256]{2,1,0:T(8,128)(2,1)} %bitcast.5, bf16[320,1280]{1,0:T(8,128)(2,1)} %bitcast.4, ...), custom_call_target="tpu_custom_call" | custom-call | tf_op jit(solution)/shard_map/pallas_call | solution.py:420
  62.3 2.5 %shard_map.120 = (bf16[64,1280]{1,0:T(8,128)(2,1)}, f32[160,320]{1,0:T(8,128)}, f32[160,320]{1,0:T(8,128)}, f32[160,640]{1,0:T(8,128)}, f32[160,640]{1,0:T(8,128)}) custom-call(bf16[64,1280]{1,0:T(8,128)(2,1)} %get-tuple-element.13.in_grad, f32[160,1280]{1,0:T(8,128)} %get-tuple-element.14.mlp_sum, f32[160,640]{1,0:T(8,128)} %get-tuple-element.15.att_sum), custom_call_target="tpu_custom_call" | custom-call | tf_op jit(solution)/shard_map/pallas_call | solution.py:472
